TPU v7x, 128 devices: a whole 4x4x4 slice. The times are simulated.
128 devices in a mesh: dp: 8 (over x, core), feat: 16 (over z, y).
Axes of the slice: x: 4, y: 4, z: 4, core: 2. Of those that a mesh axis runs over, the one named last changes fastest.
Arguments:
- features: bfloat16 [12288, 65536], P('dp', 'feat'), may hold values from -64 to 64
- weight: float32 [16, 65536], P(None, 'feat'), may hold values from -1 to 1
- labels: int32 [12288], P('dp'), may hold values from 0 to 15
- sample_weight: int32 [12288], P('dp'), may hold values from 1 to 4
Outputs:
- logit_step: float32 [12288, 16], P('dp')
- mean_loss: float32 [], replicated
All inputs are finite; a program needn't handle non-finite values.
Results may differ from a plain program's by a relative error of at most 0.014.
Values may be sent and summed in bfloat16 or wider, within the bound.
A program may use at most 64 MiB of HBM per device.

v0:
```python
import jax
import jax.numpy as jnp
from jax import lax
from jax.sharding import PartitionSpec as P

CG_ITERS = 4
RIDGE_COEF = 0.1
NORM_GUARD = 1e-06


def row_products(features, matrix_b):
    return lax.dot_general(
        features, matrix_b, (((1,), (1,)), ((), ())), preferred_element_type=jnp.float32
    )


def column_products(rows_b, features):
    return lax.dot_general(
        rows_b, features, (((0,), (0,)), ((), ())), preferred_element_type=jnp.float32
    )


def on_device(features, weight, labels, sample_weight):
    classes = weight.shape[0]
    weight_b = weight.astype(jnp.bfloat16)
    logits = lax.psum(row_products(features, weight_b), "feat")
    row_top = jnp.max(logits, axis=1, keepdims=True)
    shifted = jnp.exp(logits - row_top)
    summed = jnp.sum(shifted, axis=1, keepdims=True)
    class_prob = shifted / summed
    log_total = row_top[:, 0] + jnp.log(summed[:, 0])
    row_weight = sample_weight.astype(jnp.float32)
    onehot = (labels[:, None] == jnp.arange(classes, dtype=jnp.int32)[None, :]).astype(jnp.float32)
    picked = jnp.sum(logits * onehot, axis=1)
    weight_total, loss_total = lax.psum(
        (jnp.sum(row_weight), jnp.sum(row_weight * (log_total - picked))), "dp"
    )
    mean_loss = loss_total / weight_total
    row_scale = (row_weight / weight_total)[:, None]
    resid_rows = (row_scale * (class_prob - onehot)).astype(jnp.bfloat16)
    grad_partial = column_products(resid_rows, features)

    def inner_total(value):
        return lax.psum(value, "feat")

    gradient = (
        lax.psum(grad_partial.astype(jnp.bfloat16), "dp").astype(jnp.float32) + RIDGE_COEF * weight
    )
    newton_step = jnp.zeros_like(gradient)
    residual = -gradient
    direction = residual
    res_norm = inner_total(jnp.sum(residual * residual))
    for _ in range(CG_ITERS):
        direction_b = direction.astype(jnp.bfloat16)
        dir_scores = lax.psum(
            row_products(features, direction_b).astype(jnp.bfloat16), "feat"
        ).astype(jnp.float32)
        mixed_mean = jnp.sum(class_prob * dir_scores, axis=1, keepdims=True)
        curv_rows = (row_scale * class_prob * (dir_scores - mixed_mean)).astype(jnp.bfloat16)
        hess_image = (
            lax.psum(column_products(curv_rows, features).astype(jnp.bfloat16), "dp").astype(
                jnp.float32
            )
            + RIDGE_COEF * direction
        )
        step_size = res_norm / inner_total(jnp.sum(direction * hess_image))
        newton_step = newton_step + step_size * direction
        residual = residual - step_size * hess_image
        new_norm = inner_total(jnp.sum(residual * residual))
        direction = residual + new_norm / (res_norm + NORM_GUARD) * direction
        res_norm = new_norm
    step_b = newton_step.astype(jnp.bfloat16)
    logit_step = lax.psum(row_products(features, step_b).astype(jnp.bfloat16), "feat").astype(
        jnp.float32
    )
    return (logit_step, mean_loss)


def solution(mesh):
    in_specs = (P("dp", "feat"), P(None, "feat"), P("dp"), P("dp"))
    out_specs = (P("dp", None), P())
    return jax.shard_map(
        on_device, mesh=mesh, in_specs=in_specs, out_specs=out_specs, check_vma=False
    )
```

profile of v0, /device:TPU:0, one launch (start us, length us, event | category | flops | bytes accessed | tf_op | source)
XLA Modules:
  0.0 1117.8 jit_solution(13051484265639094176)
XLA Ops:
  7.2 0.0 copy-start.5
  7.2 0.0 copy-start.6
  7.2 0.0 all-reduce.8.cloned.1.call-start
  7.2 1.3 convert_reduce_fusion
  8.5 8.6 fusion.12
  17.1 0.0 all-reduce.8.cloned.1.call-update
  17.1 0.0 all-reduce.10.cloned.1.call-start
  17.2 15.4 %psum.147 = f32[]{:T(128)} all-reduce(f32[]{:T(128)} %convert_reduce_fusion), channel_id=1, replica_groups=mesh['dp'=8,'feat'=16] {'dp'}, use_global_device_ids=true, to_apply=%region_1.0 | all-reduce | flops 1 | bytes 8 | tf_op jit(solution)/shard_map/psum | solution.py:35
  32.5 0.0 copy-done.5
  32.5 0.6 convert_divide_fusion
  33.2 69.7 %all-reduce.8.cloned.1.call-done = f32[1536,16]{0,1:T(8,128)} async-done(((f32[1536,16]{0,1:T(8,128)}), f32[1536,16]{0,1:T(8,128)}) %all-reduce.8.cloned.1.call-update) | async-done | bytes 98320 | tf_op jit(solution)/shard_map/psum | solution.py:26
  102.9 0.9 reduce_max.9
  103.8 0.9 fusion.27
  104.8 0.0 copy-done.6
  104.8 0.0 copy-start
  104.8 7.1 convolution_convert_fusion.4
  111.9 0.0 all-reduce.10.cloned.1.call-update
  111.9 0.0 all-reduce.12.cloned.1.call-start
  111.9 58.6 %all-reduce.10.cloned.1.call-done = bf16[16,4096]{1,0:T(8,128)(2,1)} async-done(((bf16[16,4096]{1,0:T(8,128)(2,1)}), bf16[16,4096]{1,0:T(8,128)(2,1)}) %all-reduce.10.cloned.1.call-update) | async-done | bytes 131088 | tf_op jit(solution)/shard_map/psum | solution.py:47
  170.5 0.0 copy-done.4
  170.5 0.9 multiply_add_fusion.6
  171.5 7.9 fusion
  179.4 74.6 %psum.151 = bf16[1536,16]{0,1:T(8,128)(2,1)S(1)} all-reduce(bf16[1536,16]{0,1:T(8,128)(2,1)S(1)} %fusion), channel_id=1, replica_groups=mesh['dp'=8,'feat'=16] {'feat'}, use_global_device_ids=true, to_apply=%region_8.0 | all-reduce | flops 24576 | bytes 98304 | tf_op jit(solution)/shard_map/psum | solution.py:55
  254.0 0.1 select_reduce_fusion
  254.1 7.0 convolution_convert_fusion.3
  261.1 0.0 all-reduce.12.cloned.1.call-update
  261.1 0.0 all-reduce.14.cloned.1.call-start
  261.1 53.6 %all-reduce.12.cloned.1.call-done = bf16[16,4096]{1,0:T(8,128)(2,1)} async-done(((bf16[16,4096]{1,0:T(8,128)(2,1)}), bf16[16,4096]{1,0:T(8,128)(2,1)}) %all-reduce.12.cloned.1.call-update) | async-done | bytes 131088 | tf_op jit(solution)/shard_map/psum | solution.py:61
  314.7 1.6 multiply_reduce_fusion.6
  316.3 41.3 %all-reduce = (f32[]{:T(128)}, f32[]{:T(128)}) all-reduce(f32[]{:T(128)} %get-tuple-element.3, f32[]{:T(128)} %get-tuple-element.2), channel_id=1, replica_groups=mesh['dp'=8,'feat'=16] {'feat'}, use_global_device_ids=true, to_apply=%region_7.0 | all-reduce | flops 2 | bytes 16 | tf_op jit(solution)/shard_map/psum | solution.py:44
  359.0 1.6 multiply_reduce_fusion.5
  361.2 36.3 %psum.154 = f32[]{:T(128)} all-reduce(f32[]{:T(128)} %multiply_reduce_fusion.5), channel_id=1, replica_groups=mesh['dp'=8,'feat'=16] {'feat'}, use_global_device_ids=true, to_apply=%region_14.0 | all-reduce | flops 1 | bytes 8 | tf_op jit(solution)/shard_map/psum | solution.py:44
  398.2 8.0 fusion.1
  406.2 71.7 %psum.155 = bf16[1536,16]{0,1:T(8,128)(2,1)S(1)} all-reduce(bf16[1536,16]{0,1:T(8,128)(2,1)S(1)} %fusion.1), channel_id=1, replica_groups=mesh['dp'=8,'feat'=16] {'feat'}, use_global_device_ids=true, to_apply=%region_15.0 | all-reduce | flops 24576 | bytes 98304 | tf_op jit(solution)/shard_map/psum | solution.py:55
  477.9 7.0 convolution_convert_fusion.2
  484.9 0.0 all-reduce.14.cloned.1.call-update
  484.9 0.0 all-reduce.16.cloned.1.call-start
  484.9 53.6 %all-reduce.14.cloned.1.call-done = bf16[16,4096]{1,0:T(8,128)(2,1)} async-done(((bf16[16,4096]{1,0:T(8,128)(2,1)}), bf16[16,4096]{1,0:T(8,128)(2,1)}) %all-reduce.14.cloned.1.call-update) | async-done | bytes 131088 | tf_op jit(solution)/shard_map/psum | solution.py:61
  538.5 1.7 multiply_reduce_fusion.4
  540.2 41.3 %psum.157 = f32[]{:T(128)} all-reduce(f32[]{:T(128)} %multiply_reduce_fusion.4), channel_id=1, replica_groups=mesh['dp'=8,'feat'=16] {'feat'}, use_global_device_ids=true, to_apply=%region_19.0 | all-reduce | flops 1 | bytes 8 | tf_op jit(solution)/shard_map/psum | solution.py:44
  582.9 1.7 multiply_reduce_fusion.3
  585.2 36.0 %psum.158 = f32[]{:T(128)} all-reduce(f32[]{:T(128)} %multiply_reduce_fusion.3), channel_id=1, replica_groups=mesh['dp'=8,'feat'=16] {'feat'}, use_global_device_ids=true, to_apply=%region_21.0 | all-reduce | flops 1 | bytes 8 | tf_op jit(solution)/shard_map/psum | solution.py:44
  621.9 8.0 fusion.2
  629.9 71.7 %psum.159 = bf16[1536,16]{0,1:T(8,128)(2,1)S(1)} all-reduce(bf16[1536,16]{0,1:T(8,128)(2,1)S(1)} %fusion.2), channel_id=1, replica_groups=mesh['dp'=8,'feat'=16] {'feat'}, use_global_device_ids=true, to_apply=%region_22.0 | all-reduce | flops 24576 | bytes 98304 | tf_op jit(solution)/shard_map/psum | solution.py:55
  701.6 7.0 convolution_convert_fusion.1
  708.6 0.0 all-reduce.16.cloned.1.call-update
  708.6 0.0 all-reduce.18.cloned.1.call-start
  708.6 53.6 %all-reduce.16.cloned.1.call-done = bf16[16,4096]{1,0:T(8,128)(2,1)} async-done(((bf16[16,4096]{1,0:T(8,128)(2,1)}), bf16[16,4096]{1,0:T(8,128)(2,1)}) %all-reduce.16.cloned.1.call-update) | async-done | bytes 131088 | tf_op jit(solution)/shard_map/psum | solution.py:61
  762.3 1.7 multiply_reduce_fusion.2
  763.9 41.2 %psum.161 = f32[]{:T(128)} all-reduce(f32[]{:T(128)} %multiply_reduce_fusion.2), channel_id=1, replica_groups=mesh['dp'=8,'feat'=16] {'feat'}, use_global_device_ids=true, to_apply=%region_26.0 | all-reduce | flops 1 | bytes 8 | tf_op jit(solution)/shard_map/psum | solution.py:44
  806.4 1.7 multiply_reduce_fusion.1
  808.7 36.2 %psum.162 = f32[]{:T(128)} all-reduce(f32[]{:T(128)} %multiply_reduce_fusion.1), channel_id=1, replica_groups=mesh['dp'=8,'feat'=16] {'feat'}, use_global_device_ids=true, to_apply=%region_28.0 | all-reduce | flops 1 | bytes 8 | tf_op jit(solution)/shard_map/psum | solution.py:44
  845.6 8.0 fusion.3
  853.6 71.7 %psum.163 = bf16[1536,16]{0,1:T(8,128)(2,1)S(1)} all-reduce(bf16[1536,16]{0,1:T(8,128)(2,1)S(1)} %fusion.3), channel_id=1, replica_groups=mesh['dp'=8,'feat'=16] {'feat'}, use_global_device_ids=true, to_apply=%region_29.0 | all-reduce | flops 24576 | bytes 98304 | tf_op jit(solution)/shard_map/psum | solution.py:55
  925.3 7.0 convolution_convert_fusion
  932.3 0.0 all-reduce.18.cloned.1.call-update
  932.3 0.7 multiply_reduce_fusion.8
  933.0 13.1 %psum.167 = f32[]{:T(128)} all-reduce(f32[]{:T(128)} %multiply_reduce_fusion.8), channel_id=1, replica_groups=mesh['dp'=8,'feat'=16] {'dp'}, use_global_device_ids=true, to_apply=%region_37.0 | all-reduce | flops 1 | bytes 8 | tf_op jit(solution)/shard_map/psum | solution.py:35
  946.1 39.8 %all-reduce.18.cloned.1.call-done = bf16[16,4096]{1,0:T(8,128)(2,1)} async-done(((bf16[16,4096]{1,0:T(8,128)(2,1)}), bf16[16,4096]{1,0:T(8,128)(2,1)}) %all-reduce.18.cloned.1.call-update) | async-done | bytes 131088 | tf_op jit(solution)/shard_map/psum | solution.py:61
  985.9 1.8 multiply_reduce_fusion
  989.1 41.2 %psum.165 = f32[]{:T(128)} all-reduce(f32[]{:T(128)} %multiply_reduce_fusion), channel_id=1, replica_groups=mesh['dp'=8,'feat'=16] {'feat'}, use_global_device_ids=true, to_apply=%region_33.0 | all-reduce | flops 1 | bytes 8 | tf_op jit(solution)/shard_map/psum | solution.py:44
  1031.6 7.9 fusion.4
  1039.5 69.6 %psum.166 = bf16[1536,16]{0,1:T(8,128)(2,1)S(1)} all-reduce(bf16[1536,16]{0,1:T(8,128)(2,1)S(1)} %fusion.4), channel_id=1, replica_groups=mesh['dp'=8,'feat'=16] {'feat'}, use_global_device_ids=true, to_apply=%region_34.0 | all-reduce | flops 24576 | bytes 98304 | tf_op jit(solution)/shard_map/psum | solution.py:73
  1109.2 0.7 convert_element_type.151
  (11 shorter events, 0.1 us)
Async XLA Ops:
  7.2 25.4 %copy-start.5 = (s32[1536]{0:T(1024)S(1)}, s32[1536]{0:T(1024)}, u32[]{:S(2)}) copy-start(s32[1536]{0:T(1024)} %param.7) | copy-start | bytes 18436
  7.2 97.6 %copy-start.6 = (s32[1536]{0:T(1024)S(1)}, s32[1536]{0:T(1024)}, u32[]{:S(2)}) copy-start(s32[1536]{0:T(1024)} %param.6) | copy-start | bytes 18436
  7.2 95.7 %all-reduce.8.cloned.1.call-start = ((), (), s32[]{:S(2)}) async-start(), calls=%async_computation | async-start | bytes 196608 | tf_op jit(solution)/shard_map/psum | solution.py:26
  17.1 153.4 %copy-start.4 = (f32[16,4096]{1,0:T(8,128)S(1)}, f32[16,4096]{1,0:T(8,128)}, u32[]{:S(2)}) copy-start(f32[16,4096]{1,0:T(8,128)} %param.5) | copy-start | bytes 786436
  17.1 153.4 %all-reduce.10.cloned.1.call-start = ((), (), s32[]{:S(2)}) async-start(), calls=%async_computation.1 | async-start | bytes 262144 | tf_op jit(solution)/shard_map/psum | solution.py:47
  104.8 149.2 %copy-start = (f32[1536,16]{0,1:T(8,128)S(1)}, f32[1536,16]{0,1:T(8,128)}, u32[]{:S(2)}) copy-start(f32[1536,16]{0,1:T(8,128)} %all-reduce.8.cloned.1.call-done) | copy-start | bytes 294916
  111.9 202.9 %all-reduce.12.cloned.1.call-start = ((), (), s32[]{:S(2)}) async-start(), calls=%async_computation.2 | async-start | bytes 262144 | tf_op jit(solution)/shard_map/psum | solution.py:61
  261.1 277.4 %all-reduce.14.cloned.1.call-start = ((), (), s32[]{:S(2)}) async-start(), calls=%async_computation.3 | async-start | bytes 262144 | tf_op jit(solution)/shard_map/psum | solution.py:61
  406.2 132.3 %copy-start.1 = (bf16[16,4096]{1,0:T(8,128)(2,1)S(1)}, bf16[16,4096]{1,0:T(8,128)(2,1)}, u32[]{:S(2)}) copy-start(bf16[16,4096]{1,0:T(8,128)(2,1)} %all-reduce.12.cloned.1.call-done) | copy-start | bytes 393220
  484.9 277.4 %all-reduce.16.cloned.1.call-start = ((), (), s32[]{:S(2)}) async-start(), calls=%async_computation.4 | async-start | bytes 262144 | tf_op jit(solution)/shard_map/psum | solution.py:61
  629.9 132.4 %copy-start.2 = (bf16[16,4096]{1,0:T(8,128)(2,1)S(1)}, bf16[16,4096]{1,0:T(8,128)(2,1)}, u32[]{:S(2)}) copy-start(bf16[16,4096]{1,0:T(8,128)(2,1)} %all-reduce.14.cloned.1.call-done) | copy-start | bytes 393220
  708.6 277.3 %all-reduce.18.cloned.1.call-start = ((), (), s32[]{:S(2)}) async-start(), calls=%async_computation.5 | async-start | bytes 262144 | tf_op jit(solution)/shard_map/psum | solution.py:61
  853.6 132.3 %copy-start.3 = (bf16[16,4096]{1,0:T(8,128)(2,1)S(1)}, bf16[16,4096]{1,0:T(8,128)(2,1)}, u32[]{:S(2)}) copy-start(bf16[16,4096]{1,0:T(8,128)(2,1)} %all-reduce.16.cloned.1.call-done) | copy-start | bytes 393220
Sparse Core Ops, SparseCore 0:
  17.3 85.6 all-reduce.7
  112.0 58.4 all-reduce.9
  261.2 53.4 all-reduce.11
  485.0 53.4 all-reduce.13
  708.7 53.4 all-reduce.15
  932.4 53.4 all-reduce.17
where the time goes:
time: 1120 us
  blocking collectives  661 us (59%)
  waiting for transfers between devices  329 us (29%)
  matrix products  83.4 us (7%)
  between operations  26 us (2%)
  other arithmetic  18 us (2%)
    psum x4, blocking collectives, on_device(): lax.psum(row_products(features, direction_b).astype(jnp.bfloat16), 'feat')  290 us
    psum x7, blocking collectives, inner_total(): return lax.psum(value, 'feat')  273 us
    psum x4, waiting for transfers between devices, on_device(): lax.psum(column_products(curv_rows, features).astype(jnp.bfloat16), 'dp')  201 us
    psum x1, waiting for transfers between devices, on_device(): logits = lax.psum(row_products(features, weight_b), 'feat')  69.7 us
    psum x1, blocking collectives, on_device(): lax.psum(row_products(features, step_b).astype(jnp.bfloat16), 'feat')  69.6 us
    psum x1, waiting for transfers between devices, on_device(): lax.psum(grad_partial.astype(jnp.bfloat16), 'dp').astype(jnp.float32)  58.6 us
    dot_general x6, matrix products, row_products(): lax.dot_general(features, matrix_b, (((1,), (1,)), ((), ())), preferred_e...  48.4 us
    dot_general x5, matrix products, column_products(): lax.dot_general(rows_b, features, (((0,), (0,)), ((), ())), preferred_ele...  35 us
  transfers between devices with their start and end apart: 6, of which 6 were waited for; matrix products, arithmetic and copies ran while one was open for 0% of the time, Pallas kernels for 0%

commit v1 on v0

--- a/solution.py
+++ b/solution.py
@@ -23,7 +23,9 @@
 def on_device(features, weight, labels, sample_weight):
     classes = weight.shape[0]
     weight_b = weight.astype(jnp.bfloat16)
-    logits = lax.psum(row_products(features, weight_b), "feat")
+    part = row_products(features, weight_b)
+    blocks = lax.all_gather(part, "feat")
+    logits = jnp.sum(blocks, axis=0)
     row_top = jnp.max(logits, axis=1, keepdims=True)
     shifted = jnp.exp(logits - row_top)
     summed = jnp.sum(shifted, axis=1, keepdims=True)

time: 1120 us -> 1080 us (0.964)
  waiting for transfers between devices: 329 us -> 290 us
    psum x1 -> x0, waiting for transfers between devices: 69.7 us -> none  [on_device(): logits = lax.psum(row_products(features, weight_b), 'feat')]
    all_gather x0 -> x1, waiting for transfers between devices: none -> 29.8 us  [on_device(): blocks = lax.all_gather(part, 'feat')]
where the time goes in v1:
time: 1080 us
  blocking collectives  661 us (61%)
  waiting for transfers between devices  290 us (27%)
  matrix products  83.3 us (8%)
  between operations  26 us (2%)
  other arithmetic  15.8 us (1%)
    psum x4, blocking collectives, on_device(): lax.psum(row_products(features, direction_b).astype(jnp.bfloat16), 'feat')  290 us
    psum x7, blocking collectives, inner_total(): return lax.psum(value, 'feat')  273 us
    psum x4, waiting for transfers between devices, on_device(): lax.psum(column_products(curv_rows, features).astype(jnp.bfloat16), 'dp')  201 us
    psum x1, blocking collectives, on_device(): lax.psum(row_products(features, step_b).astype(jnp.bfloat16), 'feat')  69.6 us
    psum x1, waiting for transfers between devices, on_device(): lax.psum(grad_partial.astype(jnp.bfloat16), 'dp').astype(jnp.float32)  59.2 us
    dot_general x6, matrix products, row_products(): lax.dot_general(features, matrix_b, (((1,), (1,)), ((), ())), preferred_e...  48.4 us
    dot_general x5, matrix products, column_products(): lax.dot_general(rows_b, features, (((0,), (0,)), ((), ())), preferred_ele...  34.9 us
    all_gather x1, waiting for transfers between devices, on_device(): blocks = lax.all_gather(part, 'feat')  29.8 us
  transfers between devices with their start and end apart: 6, of which 6 were waited for; matrix products, arithmetic and copies ran while one was open for 0% of the time, Pallas kernels for 0%

profile of v1, /device:TPU:0, one launch (start us, length us, event | category | flops | bytes accessed | tf_op | source)
XLA Modules:
  0.0 1078.5 jit_solution(10470772019572565474)
XLA Ops:
  7.2 0.0 copy-start.4
  7.2 0.0 copy-start.5
  7.2 0.0 all-gather.3.cloned.1.call-start
  7.2 8.6 fusion.12
  15.8 0.0 all-gather.3.cloned.1.call-update
  15.8 0.0 all-reduce.7.cloned.1.call-start
  15.9 0.0 copy-done.4
  15.9 0.6 convert_reduce_fusion
  16.5 15.3 %psum.140 = f32[]{:T(128)} all-reduce(f32[]{:T(128)} %convert_reduce_fusion), channel_id=1, replica_groups=mesh['dp'=8,'feat'=16] {'dp'}, use_global_device_ids=true, to_apply=%region_1.0 | all-reduce | flops 1 | bytes 8 | tf_op jit(solution)/shard_map/psum | solution.py:37
  31.8 0.6 convert_divide_fusion
  32.5 29.8 %all-gather.3.cloned.1.call-done = f32[24576,16]{0,1:T(8,128)} async-done(((f32[1536,16]{0,1:T(8,128)}), f32[24576,16]{0,1:T(8,128)}) %all-gather.3.cloned.1.call-update) | async-done | bytes 1572880 | tf_op jit(solution)/shard_map/all_gather | solution.py:27
  62.3 2.3 copy.6
  64.6 0.2 bitcast_reduce_fusion
  65.0 0.0 copy-done.5
  65.0 7.0 convolution_convert_fusion.4
  71.9 0.0 all-reduce.7.cloned.1.call-update
  72.0 0.0 all-reduce.9.cloned.1.call-start
  72.0 59.2 %all-reduce.7.cloned.1.call-done = bf16[16,4096]{1,0:T(8,128)(2,1)} async-done(((bf16[16,4096]{1,0:T(8,128)(2,1)}), bf16[16,4096]{1,0:T(8,128)(2,1)}) %all-reduce.7.cloned.1.call-update) | async-done | bytes 131088 | tf_op jit(solution)/shard_map/psum | solution.py:49
  131.2 0.0 copy-done.3
  131.2 0.9 multiply_add_fusion.6
  132.1 7.9 fusion
  140.1 74.6 %psum.143 = bf16[1536,16]{0,1:T(8,128)(2,1)S(1)} all-reduce(bf16[1536,16]{0,1:T(8,128)(2,1)S(1)} %fusion), channel_id=1, replica_groups=mesh['dp'=8,'feat'=16] {'feat'}, use_global_device_ids=true, to_apply=%region_8.0 | all-reduce | flops 24576 | bytes 98304 | tf_op jit(solution)/shard_map/psum | solution.py:57
  214.7 0.1 select_reduce_fusion
  214.8 7.0 convolution_convert_fusion.3
  221.8 0.0 all-reduce.9.cloned.1.call-update
  221.8 0.0 all-reduce.11.cloned.1.call-start
  221.8 53.6 %all-reduce.9.cloned.1.call-done = bf16[16,4096]{1,0:T(8,128)(2,1)} async-done(((bf16[16,4096]{1,0:T(8,128)(2,1)}), bf16[16,4096]{1,0:T(8,128)(2,1)}) %all-reduce.9.cloned.1.call-update) | async-done | bytes 131088 | tf_op jit(solution)/shard_map/psum | solution.py:63
  275.4 1.6 multiply_reduce_fusion.6
  277.0 41.3 %all-reduce = (f32[]{:T(128)}, f32[]{:T(128)}) all-reduce(f32[]{:T(128)} %get-tuple-element.3, f32[]{:T(128)} %get-tuple-element.2), channel_id=1, replica_groups=mesh['dp'=8,'feat'=16] {'feat'}, use_global_device_ids=true, to_apply=%region_7.0 | all-reduce | flops 2 | bytes 16 | tf_op jit(solution)/shard_map/psum | solution.py:46
  319.6 1.6 multiply_reduce_fusion.5
  321.2 36.3 %psum.146 = f32[]{:T(128)} all-reduce(f32[]{:T(128)} %multiply_reduce_fusion.5), channel_id=1, replica_groups=mesh['dp'=8,'feat'=16] {'feat'}, use_global_device_ids=true, to_apply=%region_14.0 | all-reduce | flops 1 | bytes 8 | tf_op jit(solution)/shard_map/psum | solution.py:46
  358.8 8.0 fusion.1
  366.8 71.7 %psum.147 = bf16[1536,16]{0,1:T(8,128)(2,1)S(1)} all-reduce(bf16[1536,16]{0,1:T(8,128)(2,1)S(1)} %fusion.1), channel_id=1, replica_groups=mesh['dp'=8,'feat'=16] {'feat'}, use_global_device_ids=true, to_apply=%region_15.0 | all-reduce | flops 24576 | bytes 98304 | tf_op jit(solution)/shard_map/psum | solution.py:57
  438.5 7.0 convolution_convert_fusion.2
  445.5 0.0 all-reduce.11.cloned.1.call-update
  445.5 0.0 all-reduce.13.cloned.1.call-start
  445.6 53.6 %all-reduce.11.cloned.1.call-done = bf16[16,4096]{1,0:T(8,128)(2,1)} async-done(((bf16[16,4096]{1,0:T(8,128)(2,1)}), bf16[16,4096]{1,0:T(8,128)(2,1)}) %all-reduce.11.cloned.1.call-update) | async-done | bytes 131088 | tf_op jit(solution)/shard_map/psum | solution.py:63
  499.2 0.0 copy-done
  499.2 1.7 multiply_reduce_fusion.4
  500.9 41.3 %psum.149 = f32[]{:T(128)} all-reduce(f32[]{:T(128)} %multiply_reduce_fusion.4), channel_id=1, replica_groups=mesh['dp'=8,'feat'=16] {'feat'}, use_global_device_ids=true, to_apply=%region_19.0 | all-reduce | flops 1 | bytes 8 | tf_op jit(solution)/shard_map/psum | solution.py:46
  543.5 1.7 multiply_reduce_fusion.3
  545.9 36.0 %psum.150 = f32[]{:T(128)} all-reduce(f32[]{:T(128)} %multiply_reduce_fusion.3), channel_id=1, replica_groups=mesh['dp'=8,'feat'=16] {'feat'}, use_global_device_ids=true, to_apply=%region_21.0 | all-reduce | flops 1 | bytes 8 | tf_op jit(solution)/shard_map/psum | solution.py:46
  582.5 8.0 fusion.2
  590.5 71.7 %psum.151 = bf16[1536,16]{0,1:T(8,128)(2,1)S(1)} all-reduce(bf16[1536,16]{0,1:T(8,128)(2,1)S(1)} %fusion.2), channel_id=1, replica_groups=mesh['dp'=8,'feat'=16] {'feat'}, use_global_device_ids=true, to_apply=%region_22.0 | all-reduce | flops 24576 | bytes 98304 | tf_op jit(solution)/shard_map/psum | solution.py:57
  662.2 7.0 convolution_convert_fusion.1
  669.2 0.0 all-reduce.13.cloned.1.call-update
  669.2 0.0 all-reduce.15.cloned.1.call-start
  669.3 53.6 %all-reduce.13.cloned.1.call-done = bf16[16,4096]{1,0:T(8,128)(2,1)} async-done(((bf16[16,4096]{1,0:T(8,128)(2,1)}), bf16[16,4096]{1,0:T(8,128)(2,1)}) %all-reduce.13.cloned.1.call-update) | async-done | bytes 131088 | tf_op jit(solution)/shard_map/psum | solution.py:63
  722.9 1.7 multiply_reduce_fusion.2
  724.6 41.2 %psum.153 = f32[]{:T(128)} all-reduce(f32[]{:T(128)} %multiply_reduce_fusion.2), channel_id=1, replica_groups=mesh['dp'=8,'feat'=16] {'feat'}, use_global_device_ids=true, to_apply=%region_26.0 | all-reduce | flops 1 | bytes 8 | tf_op jit(solution)/shard_map/psum | solution.py:46
  767.0 1.7 multiply_reduce_fusion.1
  769.4 36.2 %psum.154 = f32[]{:T(128)} all-reduce(f32[]{:T(128)} %multiply_reduce_fusion.1), channel_id=1, replica_groups=mesh['dp'=8,'feat'=16] {'feat'}, use_global_device_ids=true, to_apply=%region_28.0 | all-reduce | flops 1 | bytes 8 | tf_op jit(solution)/shard_map/psum | solution.py:46
  806.2 8.0 fusion.3
  814.2 71.7 %psum.155 = bf16[1536,16]{0,1:T(8,128)(2,1)S(1)} all-reduce(bf16[1536,16]{0,1:T(8,128)(2,1)S(1)} %fusion.3), channel_id=1, replica_groups=mesh['dp'=8,'feat'=16] {'feat'}, use_global_device_ids=true, to_apply=%region_29.0 | all-reduce | flops 24576 | bytes 98304 | tf_op jit(solution)/shard_map/psum | solution.py:57
  885.9 7.0 convolution_convert_fusion
  892.9 0.0 all-reduce.15.cloned.1.call-update
  892.9 0.7 multiply_reduce_fusion.8
  893.6 13.1 %psum.159 = f32[]{:T(128)} all-reduce(f32[]{:T(128)} %multiply_reduce_fusion.8), channel_id=1, replica_groups=mesh['dp'=8,'feat'=16] {'dp'}, use_global_device_ids=true, to_apply=%region_37.0 | all-reduce | flops 1 | bytes 8 | tf_op jit(solution)/shard_map/psum | solution.py:37
  906.7 39.8 %all-reduce.15.cloned.1.call-done = bf16[16,4096]{1,0:T(8,128)(2,1)} async-done(((bf16[16,4096]{1,0:T(8,128)(2,1)}), bf16[16,4096]{1,0:T(8,128)(2,1)}) %all-reduce.15.cloned.1.call-update) | async-done | bytes 131088 | tf_op jit(solution)/shard_map/psum | solution.py:63
  946.6 1.8 multiply_reduce_fusion
  949.7 41.2 %psum.157 = f32[]{:T(128)} all-reduce(f32[]{:T(128)} %multiply_reduce_fusion), channel_id=1, replica_groups=mesh['dp'=8,'feat'=16] {'feat'}, use_global_device_ids=true, to_apply=%region_33.0 | all-reduce | flops 1 | bytes 8 | tf_op jit(solution)/shard_map/psum | solution.py:46
  992.3 7.9 fusion.4
  1000.2 69.6 %psum.158 = bf16[1536,16]{0,1:T(8,128)(2,1)S(1)} all-reduce(bf16[1536,16]{0,1:T(8,128)(2,1)S(1)} %fusion.4), channel_id=1, replica_groups=mesh['dp'=8,'feat'=16] {'feat'}, use_global_device_ids=true, to_apply=%region_34.0 | all-reduce | flops 24576 | bytes 98304 | tf_op jit(solution)/shard_map/psum | solution.py:75
  1069.8 0.7 convert_element_type.151
  (11 shorter events, 0.2 us)
Async XLA Ops:
  7.2 8.7 copy-start.4
  7.2 57.8 %copy-start.5 = (s32[1536]{0:T(1024)S(1)}, s32[1536]{0:T(1024)}, u32[]{:S(2)}) copy-start(s32[1536]{0:T(1024)} %param.6) | copy-start | bytes 18436
  7.2 55.1 %all-gather.3.cloned.1.call-start = ((), (), s32[]{:S(2)}) async-start(), calls=%async_computation.5 | async-start | bytes 1671168 | tf_op jit(solution)/shard_map/all_gather | solution.py:27
  15.8 115.4 %copy-start.3 = (f32[16,4096]{1,0:T(8,128)S(1)}, f32[16,4096]{1,0:T(8,128)}, u32[]{:S(2)}) copy-start(f32[16,4096]{1,0:T(8,128)} %param.5) | copy-start | bytes 786436
  15.8 115.4 %all-reduce.7.cloned.1.call-start = ((), (), s32[]{:S(2)}) async-start(), calls=%async_computation | async-start | bytes 262144 | tf_op jit(solution)/shard_map/psum | solution.py:49
  72.0 203.5 %all-reduce.9.cloned.1.call-start = ((), (), s32[]{:S(2)}) async-start(), calls=%async_computation.1 | async-start | bytes 262144 | tf_op jit(solution)/shard_map/psum | solution.py:63
  221.8 277.4 %all-reduce.11.cloned.1.call-start = ((), (), s32[]{:S(2)}) async-start(), calls=%async_computation.2 | async-start | bytes 262144 | tf_op jit(solution)/shard_map/psum | solution.py:63
  366.8 132.3 %copy-start = (bf16[16,4096]{1,0:T(8,128)(2,1)S(1)}, bf16[16,4096]{1,0:T(8,128)(2,1)}, u32[]{:S(2)}) copy-start(bf16[16,4096]{1,0:T(8,128)(2,1)} %all-reduce.9.cloned.1.call-done) | copy-start | bytes 393220
  445.5 277.4 %all-reduce.13.cloned.1.call-start = ((), (), s32[]{:S(2)}) async-start(), calls=%async_computation.3 | async-start | bytes 262144 | tf_op jit(solution)/shard_map/psum | solution.py:63
  590.5 132.4 %copy-start.1 = (bf16[16,4096]{1,0:T(8,128)(2,1)S(1)}, bf16[16,4096]{1,0:T(8,128)(2,1)}, u32[]{:S(2)}) copy-start(bf16[16,4096]{1,0:T(8,128)(2,1)} %all-reduce.11.cloned.1.call-done) | copy-start | bytes 393220
  669.2 277.3 %all-reduce.15.cloned.1.call-start = ((), (), s32[]{:S(2)}) async-start(), calls=%async_computation.4 | async-start | bytes 262144 | tf_op jit(solution)/shard_map/psum | solution.py:63
  814.2 132.3 %copy-start.2 = (bf16[16,4096]{1,0:T(8,128)(2,1)S(1)}, bf16[16,4096]{1,0:T(8,128)(2,1)}, u32[]{:S(2)}) copy-start(bf16[16,4096]{1,0:T(8,128)(2,1)} %all-reduce.13.cloned.1.call-done) | copy-start | bytes 393220
Sparse Core Ops, SparseCore 0:
  16.0 46.3 all-gather.2
  72.1 59.0 all-reduce.6
  221.9 53.4 all-reduce.8
  445.7 53.4 all-reduce.10
  669.4 53.4 all-reduce.12
  893.1 53.4 all-reduce.14
